TPU v7x, 512 devices: a whole 4x8x8 slice. The times are simulated.
512 devices in a mesh: seq: 64 (over y_lo, z, x), fsdp: 8 (over y_hi, core).
Axes of the slice: x: 4, y: 8 (y_hi: 4, y_lo: 2; y = y_hi * 2 + y_lo), z: 8, core: 2. Of those that a mesh axis runs over, the one named last changes fastest.
Arguments:
- features: bfloat16 [8, 8192, 6144], P('fsdp', 'seq'), may hold values from -6 to 6
- short_taps: float32 [7, 384], replicated, may hold values from -2 to 2
- long_taps: float32 [128, 128], replicated, may hold values from -0.5 to 0.5
- out_weight: bfloat16 [2048, 4096], P(None, 'fsdp'), may hold values from -0.125 to 0.125
Outputs:
- mixer_out: bfloat16 [8, 8192, 4096], P('fsdp', 'seq')
All inputs are finite; a program needn't handle non-finite values.
Results may differ from a plain program's by a relative error of at most 0.0057.
Values may be sent and summed in bfloat16 or wider, within the bound.
A program may use at most 128 MiB of HBM per device.

v0:
```python
import jax
import jax.numpy as jnp
from jax import lax
from jax.sharding import PartitionSpec as P

GROUP = 16


def passed_along(block, axis, distance):
    devices = range(lax.axis_size(axis))
    route = [(i - distance, i) for i in devices if i - distance in devices]
    return lax.ppermute(block, axis, route)


def long_filter(joined, long_taps, row_count):
    tap_count = long_taps.shape[0]
    group_count = long_taps.shape[1]
    span = joined.shape[0]
    lag_table = (
        jnp.arange(row_count, dtype=jnp.int32)[:, None]
        + (tap_count - 1)
        - jnp.arange(span, dtype=jnp.int32)[None, :]
    )
    valid = (lag_table >= 0) & (lag_table < tap_count)
    safe_lag = jnp.clip(lag_table, 0, tap_count - 1)
    block_groups = min(group_count, 32)
    block_count = group_count // block_groups
    taps_blocks = long_taps.T.reshape(block_count, block_groups, tap_count)
    rows_blocks = joined.reshape(span, block_count, block_groups, GROUP).transpose(1, 0, 2, 3)

    def one_block(pair):
        taps_block, rows_block = pair
        toeplitz = jnp.where(valid[None], taps_block[:, safe_lag], jnp.float32(0.0))
        return jnp.einsum(
            "gts,sgk->tgk",
            toeplitz,
            rows_block.astype(jnp.float32),
            precision=lax.Precision.HIGHEST,
        )

    outputs = lax.map(one_block, (taps_blocks, rows_blocks))
    return outputs.transpose(1, 0, 2, 3).reshape(row_count, group_count * GROUP)


def on_device(features, short_taps, long_taps, out_weight):
    row_count = features.shape[1]
    channels = features.shape[2] // 3
    short_count = short_taps.shape[0]
    tap_count = long_taps.shape[0]
    edge_rows = passed_along(features[:, row_count - (short_count - 1) :, :], "seq", 1)
    extended = jnp.concatenate([edge_rows, features], axis=1)
    short_table = jnp.repeat(short_taps, GROUP, axis=1)
    filtered = jnp.zeros((features.shape[0], row_count, 3 * channels), jnp.float32)
    for index_tap in range(short_count):
        window_rows = extended[
            :, short_count - 1 - index_tap : short_count - 1 - index_tap + row_count, :
        ]
        filtered = filtered + short_table[index_tap] * window_rows.astype(jnp.float32)
    query_part = filtered[0, :, 0:channels]
    product = (
        filtered[:, :, channels : 2 * channels] * filtered[:, :, 2 * channels : 3 * channels]
    ).astype(jnp.bfloat16)
    product = lax.optimization_barrier(product)
    prior_rows = passed_along(product[:, row_count - (tap_count - 1) :, :], "seq", 1)
    joined = jnp.concatenate([prior_rows, product], axis=1)[0]
    mixed_long = long_filter(joined, long_taps, row_count)
    gated_local = (query_part * mixed_long).astype(jnp.bfloat16)
    result = jnp.dot(
        gated_local,
        lax.all_gather(out_weight, "fsdp", axis=1, tiled=True),
        preferred_element_type=jnp.float32,
    )
    return result.astype(jnp.bfloat16)[None]


def solution(mesh):
    in_specs = (P("fsdp", "seq", None), P(), P(), P(None, "fsdp"))
    out_specs = P("fsdp", "seq", None)
    return jax.shard_map(
        on_device, mesh=mesh, in_specs=in_specs, out_specs=out_specs, check_vma=False
    )
```

profile of v0, /device:TPU:56, one launch (start us, length us, event | category | flops | bytes accessed | tf_op | source)
XLA Modules:
  0.0 504.6 jit_solution(6604021708387002852)
XLA Ops:
  6.5 0.7 all-gather.2.cloned.1.call-update
  7.3 0.9 slice.86
  8.2 3.4 collective-permute-start
  11.6 1.0 slice_reduce_fusion.6
  14.3 10.6 %collective-permute-done = bf16[1,6,6144]{2,1,0:T(8,128)(2,1)S(1)} collective-permute-done((bf16[1,6,6144]{2,1,0:T(8,128)(2,1)S(1)}, bf16[1,6,6144]{2,1,0:T(8,128)(2,1)S(1)}, u32[]{:S(2)}, u32[]{:S(2)}) %collective-permute-start) | collective-permute-done | bytes 73760 | tf_op jit(solution)/shard_map/ppermute | solution.py:12
  24.9 7.2 %multiply_add_fusion = f32[1,128,6144]{2,1,0:T(8,128)S(1)} fusion(bf16[1,128,6144]{2,1,0:T(8,128)(2,1)} %param.6, bf16[1,6,6144]{2,1,0:T(8,128)(2,1)S(1)} %collective-permute-done, f32[6144]{0:T(1024)S(1)} %broadcast_in_dim.68, f32[6144]{0:T(1024)S(1)} %broadcast_in_dim.66, f32[6144]{0:T(1024)S(1)} %broadcast_in_dim.64, f32[6144]{0:T(1024)S(1)} %broadcast_in_dim.62, ...), kind=kLoop, calls=%fused_computation.28 | loop fusion | flops 29884416 | bytes 4964352 | tf_op jit(solution)/shard_map/add | solution.py:58
  32.2 0.8 copy-done
  33.0 0.9 slice.122
  33.9 2.1 collective-permute-start.1
  36.1 95.4 %collective-permute-done.1 = bf16[1,127,2048]{2,1,0:T(8,128)(2,1)} collective-permute-done((bf16[1,127,2048]{2,1,0:T(8,128)(2,1)}, bf16[1,127,2048]{2,1,0:T(8,128)(2,1)}, u32[]{:S(2)}, u32[]{:S(2)}) %collective-permute-start.1) | collective-permute-done | bytes 520224 | tf_op jit(solution)/shard_map/ppermute | solution.py:12
  131.5 2.4 pad_maximum_fusion.1
  133.9 2.3 copy.9
  136.1 349.6 %while.12 = (s32[]{:T(128)}, f32[4,128,32,16]{1,3,2,0:T(8,128)}, bf16[4,255,32,16]{1,3,2,0:T(8,128)(2,1)}, f32[4,32,128]{2,1,0:T(8,128)S(1)}, s32[128]{0:T(128)S(1)}, /*index=5*/s32[]{:T(128)}) while((s32[]{:T(128)}, f32[4,128,32,16]{1,3,2,0:T(8,128)}, bf16[4,255,32,16]{1,3,2,0:T(8,128)(2,1)}, ...), condition=%wide.region_1.2_spmd.clone.clone, body=%wide.region_0.1_spmd.clone.clone.sunk | while | flops 201911168 | bytes 30702920 | solution.py:41
  136.7 60.6 %gather_fusion = f32[32640,32]{1,0:T(8,128)} fusion(f32[32,128]{0,1:T(8,128)S(1)} %bitcast.52, s32[32768]{0:T(1024)S(1)} %pad_clamp_fusion.2), kind=kCustom, calls=%fused_computation.clone.clone.clone.1 | custom fusion | bytes 8486400 | tf_op jit(solution)/shard_map/while/body/eval_jaxpr/gather | solution.py:33
  197.3 11.5 %copy.17 = f32[32640,32]{0,1:T(8,128)} copy(f32[32640,32]{1,0:T(8,128)} %gather_fusion) | data formatting | bytes 8355840 | tf_op jit(solution)/shard_map/while/body/eval_jaxpr/gather | solution.py:33
  208.8 9.4 %reshape.112 = f32[128,255,32]{1,0,2:T(8,128)} reshape(f32[32640,32]{0,1:T(8,128)} %copy.17) | data formatting | bytes 8355840 | tf_op jit(solution)/shard_map/while/body/eval_jaxpr/gather | solution.py:33
  218.3 5.2 %fusion.40 = f32[4,128,32,16]{1,3,2,0:T(8,128)} fusion(f32[4,128,32,16]{1,3,2,0:T(8,128)} %get-tuple-element.130, s32[]{:T(128)} %get-tuple-element.129, f32[128,255,32]{1,0,2:T(8,128)} %reshape.112, pred[128,255]{1,0:T(8,128)(4,1)S(1)} %fusion.39, bf16[4,255,32,16]{1,3,2,0:T(8,128)(2,1)} %get-tuple-element.137), kind=kOutput, calls=%fused_computation.9.clone.1 | convolution fusion | flops 201584640 | bytes 4752256 | tf_op jit(solution)/shard_map/while/body/eval_jaxpr/gts,sgk->tgk/dot_general | solution.py:34
  223.7 0.3 reshape.111
  224.1 60.6 %gather_fusion = f32[32640,32]{1,0:T(8,128)} fusion(f32[32,128]{0,1:T(8,128)S(1)} %bitcast.52, s32[32768]{0:T(1024)S(1)} %pad_clamp_fusion.2), kind=kCustom, calls=%fused_computation.clone.clone.clone.1 | custom fusion | bytes 8486400 | tf_op jit(solution)/shard_map/while/body/eval_jaxpr/gather | solution.py:33
  284.7 11.5 %copy.17 = f32[32640,32]{0,1:T(8,128)} copy(f32[32640,32]{1,0:T(8,128)} %gather_fusion) | data formatting | bytes 8355840 | tf_op jit(solution)/shard_map/while/body/eval_jaxpr/gather | solution.py:33
  296.2 9.4 %reshape.112 = f32[128,255,32]{1,0,2:T(8,128)} reshape(f32[32640,32]{0,1:T(8,128)} %copy.17) | data formatting | bytes 8355840 | tf_op jit(solution)/shard_map/while/body/eval_jaxpr/gather | solution.py:33
  305.7 5.2 %fusion.40 = f32[4,128,32,16]{1,3,2,0:T(8,128)} fusion(f32[4,128,32,16]{1,3,2,0:T(8,128)} %get-tuple-element.130, s32[]{:T(128)} %get-tuple-element.129, f32[128,255,32]{1,0,2:T(8,128)} %reshape.112, pred[128,255]{1,0:T(8,128)(4,1)S(1)} %fusion.39, bf16[4,255,32,16]{1,3,2,0:T(8,128)(2,1)} %get-tuple-element.137), kind=kOutput, calls=%fused_computation.9.clone.1 | convolution fusion | flops 201584640 | bytes 4752256 | tf_op jit(solution)/shard_map/while/body/eval_jaxpr/gts,sgk->tgk/dot_general | solution.py:34
  311.5 60.6 %gather_fusion = f32[32640,32]{1,0:T(8,128)} fusion(f32[32,128]{0,1:T(8,128)S(1)} %bitcast.52, s32[32768]{0:T(1024)S(1)} %pad_clamp_fusion.2), kind=kCustom, calls=%fused_computation.clone.clone.clone.1 | custom fusion | bytes 8486400 | tf_op jit(solution)/shard_map/while/body/eval_jaxpr/gather | solution.py:33
  372.1 11.5 %copy.17 = f32[32640,32]{0,1:T(8,128)} copy(f32[32640,32]{1,0:T(8,128)} %gather_fusion) | data formatting | bytes 8355840 | tf_op jit(solution)/shard_map/while/body/eval_jaxpr/gather | solution.py:33
  383.6 9.4 %reshape.112 = f32[128,255,32]{1,0,2:T(8,128)} reshape(f32[32640,32]{0,1:T(8,128)} %copy.17) | data formatting | bytes 8355840 | tf_op jit(solution)/shard_map/while/body/eval_jaxpr/gather | solution.py:33
  393.1 5.2 %fusion.40 = f32[4,128,32,16]{1,3,2,0:T(8,128)} fusion(f32[4,128,32,16]{1,3,2,0:T(8,128)} %get-tuple-element.130, s32[]{:T(128)} %get-tuple-element.129, f32[128,255,32]{1,0,2:T(8,128)} %reshape.112, pred[128,255]{1,0:T(8,128)(4,1)S(1)} %fusion.39, bf16[4,255,32,16]{1,3,2,0:T(8,128)(2,1)} %get-tuple-element.137), kind=kOutput, calls=%fused_computation.9.clone.1 | convolution fusion | flops 201584640 | bytes 4752256 | tf_op jit(solution)/shard_map/while/body/eval_jaxpr/gts,sgk->tgk/dot_general | solution.py:34
  398.9 60.6 %gather_fusion = f32[32640,32]{1,0:T(8,128)} fusion(f32[32,128]{0,1:T(8,128)S(1)} %bitcast.52, s32[32768]{0:T(1024)S(1)} %pad_clamp_fusion.2), kind=kCustom, calls=%fused_computation.clone.clone.clone.1 | custom fusion | bytes 8486400 | tf_op jit(solution)/shard_map/while/body/eval_jaxpr/gather | solution.py:33
  459.5 11.5 %copy.17 = f32[32640,32]{0,1:T(8,128)} copy(f32[32640,32]{1,0:T(8,128)} %gather_fusion) | data formatting | bytes 8355840 | tf_op jit(solution)/shard_map/while/body/eval_jaxpr/gather | solution.py:33
  471.0 9.4 %reshape.112 = f32[128,255,32]{1,0,2:T(8,128)} reshape(f32[32640,32]{0,1:T(8,128)} %copy.17) | data formatting | bytes 8355840 | tf_op jit(solution)/shard_map/while/body/eval_jaxpr/gather | solution.py:33
  480.5 5.2 %fusion.40 = f32[4,128,32,16]{1,3,2,0:T(8,128)} fusion(f32[4,128,32,16]{1,3,2,0:T(8,128)} %get-tuple-element.130, s32[]{:T(128)} %get-tuple-element.129, f32[128,255,32]{1,0,2:T(8,128)} %reshape.112, pred[128,255]{1,0:T(8,128)(4,1)S(1)} %fusion.39, bf16[4,255,32,16]{1,3,2,0:T(8,128)(2,1)} %get-tuple-element.137), kind=kOutput, calls=%fused_computation.9.clone.1 | convolution fusion | flops 201584640 | bytes 4752256 | tf_op jit(solution)/shard_map/while/body/eval_jaxpr/gts,sgk->tgk/dot_general | solution.py:34
  485.7 2.6 copy.12
  488.3 9.4 %fusion.22 = bf16[1,128,4096]{2,1,0:T(8,128)(2,1)} fusion(bf16[2048,4096]{1,0:T(8,128)(2,1)} %all-gather.2.cloned.1.call-done, f32[128,2048]{1,0:T(8,128)} %copy.12, f32[1,128,6144]{2,1,0:T(8,128)S(1)} %multiply_add_fusion), kind=kOutput, calls=%fused_computation.22 | convolution fusion | flops 2148532224 | bytes 19922944 | tf_op jit(solution)/shard_map/dot_general | solution.py:68
  (46 shorter events, 4.1 us)
Async XLA Ops:
  6.5 481.8 %all-gather.2.cloned.1.call-start = ((), (), s32[]{:S(2)}) async-start(), calls=%async_computation | async-start | bytes 18874368 | tf_op jit(solution)/shard_map/all_gather | solution.py:70
  8.2 16.7 %collective-permute-start = (bf16[1,6,6144]{2,1,0:T(8,128)(2,1)S(1)}, bf16[1,6,6144]{2,1,0:T(8,128)(2,1)S(1)}, u32[]{:S(2)}, u32[]{:S(2)}) collective-permute-start(bf16[1,6,6144]{2,1,0:T(8,128)(2,1)S(1)} %slice.86), channel_id=1, source_target_pairs={{0,8},{8,16},{16,24},{24,32},{32,40},{40,48},{48,56},{56,64},{64,7... | collective-permute-start | bytes 221192 | tf_op jit(solution)/shard_map/ppermute | solution.py:12
  14.3 21.8 %copy-start.1 = (f32[128,128]{1,0:T(8,128)S(1)}, f32[128,128]{1,0:T(8,128)}, u32[]{:S(2)}) copy-start(f32[128,128]{1,0:T(8,128)} %param.8) | copy-start | bytes 196612
  32.2 0.8 copy-start
  33.9 97.6 %collective-permute-start.1 = (bf16[1,127,2048]{2,1,0:T(8,128)(2,1)}, bf16[1,127,2048]{2,1,0:T(8,128)(2,1)}, u32[]{:S(2)}, u32[]{:S(2)}) collective-permute-start(bf16[1,127,2048]{2,1,0:T(8,128)(2,1)} %slice.122), channel_id=1, source_target_pairs={{0,8},{8,16},{16,24},{24,32},{32,40},{40,48},{48,56},{56,64},{64,7... | collective-permute-start | bytes 1560584 | tf_op jit(solution)/shard_map/ppermute | solution.py:12
Sparse Core Ops, SparseCore 0:
  9.5 162.5 all-gather.1
where the time goes:
time: 505 us
  local copies, waits for them, and re-layouts  338 us (67%)
  waiting for transfers between devices  107 us (21%)
  matrix products  30.4 us (6%)
  between operations  13.6 us (3%)
  other arithmetic  10.5 us (2%)
  starting transfers between devices  5.49 us (1%)
    gather x12, local copies, waits for them, and re-layouts, one_block(): toeplitz = jnp.where(valid[None], taps_block[:, safe_lag], jnp.float32(0.0))  326 us
    ppermute x2, waiting for transfers between devices, passed_along(): return lax.ppermute(block, axis, route)  106 us
    dot_general x4, matrix products, one_block(): jnp.einsum('gts,sgk->tgk', toeplitz, rows_block.astype(jnp.float32), prec...  20.9 us
  transfers between devices with their start and end apart: 3, of which 2 were waited for; matrix products, arithmetic and copies ran while one was open for 73% of the time, Pallas kernels for 0%

commit v1 on v0

v1 whole, which is shorter than its diff:
```python
import functools

import jax
import jax.numpy as jnp
from jax import lax
from jax.experimental import pallas as pl
from jax.experimental.pallas import tpu as pltpu
from jax.sharding import PartitionSpec as P

MESH = pl.DeviceIdType.MESH
GROUP = 16
XN = 4
ZN = 8
LANES = 128
PIECES = 4
CHUNKS = 4
BF16 = jnp.bfloat16
F32 = jnp.float32


def kernel(
    seq_count,
    x_hbm,
    st_ref,
    lt_ref,
    w_hbm,
    out_ref,
    feat,
    fhalo,
    taps_s,
    taps_r,
    toep,
    qf,
    pown,
    phalo,
    wbuf,
    gat,
    res,
    loc_sem,
    fh_sem,
    ph_sem,
    y_sem,
    x_sem,
    g_sem,
    o_sem,
):
    rows = feat.shape[0]
    channels = qf.shape[1]
    depth = w_hbm.shape[0]
    shard = w_hbm.shape[1]
    piece = depth // PIECES
    chunk = channels // CHUNKS
    blocks = chunk // LANES
    per_block = LANES // GROUP
    half = shard // 2

    seq = lax.axis_index("seq")
    fs = lax.axis_index("fsdp")
    x = seq % XN
    z = (seq // XN) % ZN
    y_lo = seq // (XN * ZN)
    y_hi = fs // 2
    core = fs % 2
    u = x % 2
    p = z % 2
    delta = 2 * y_lo - 1
    seq_flip = seq - delta * (XN * ZN)
    hi_outer = (y_hi + delta + 4) % 4
    outer = (seq_flip, hi_outer * 2 + core)
    sibling = (seq_flip, fs)
    right = (seq - x + (x + 1) % XN, fs)
    left = (seq - x + (x + XN - 1) % XN, fs)
    seq_z = seq + XN * (1 - 2 * p)
    other = fs + 1 - 2 * core
    pool = (None, (seq, other), (seq_z, fs), (seq_z, other))
    following = (seq + 1, fs)
    previous = (seq - 1, fs)
    has_next = seq < seq_count - 1
    has_prev = seq > 0

    def remote(src, dst, send, recv, target):
        return pltpu.make_async_remote_copy(
            src_ref=src,
            dst_ref=dst,
            send_sem=send,
            recv_sem=recv,
            device_id=target,
            device_id_type=MESH,
        )

    feat_copy = pltpu.make_async_copy(x_hbm.at[0], feat, loc_sem.at[0])
    feat_copy.start()
    own_w = []
    for part in range(2):
        column = pl.multiple_of(half * p + LANES * part, LANES)
        copy = pltpu.make_async_copy(
            w_hbm.at[:, pl.ds(column, LANES)], wbuf.at[0, part], loc_sem.at[1 + part]
        )
        copy.start()
        own_w.append(copy)

    barrier = pltpu.get_barrier_semaphore()
    greeted = (outer, sibling, right, left) + pool[1:]
    greeted += (((seq + 1) % seq_count, fs), ((seq + seq_count - 1) % seq_count, fs))
    for target in greeted:
        pl.semaphore_signal(barrier, inc=1, device_id=target, device_id_type=MESH)
    pl.semaphore_wait(barrier, len(greeted))

    halo_rows = fhalo.shape[0]
    feature_halo = remote(
        x_hbm.at[0, pl.ds(rows - halo_rows, halo_rows)],
        fhalo,
        fh_sem.at[0],
        fh_sem.at[1],
        following,
    )

    @pl.when(has_next)
    def _():
        feature_halo.start()

    def y_copy(slot, k):
        at_rows = pl.ds(piece * k, piece)
        if slot == 1:
            column = pl.multiple_of(half * p + LANES * u, LANES)
            src = w_hbm.at[at_rows, pl.ds(column, LANES)]
        else:
            src = wbuf.at[slot - 1, u, at_rows]
        return remote(
            src,
            wbuf.at[slot, u, at_rows],
            y_sem.at[0, slot - 1, k],
            y_sem.at[1, slot - 1, k],
            sibling if slot == 2 else outer,
        )

    def x_copy(slot, k):
        at_rows = pl.ds(piece * k, piece)
        block = wbuf.at[slot, u, at_rows]
        return remote(
            block,
            block,
            x_sem.at[0, slot - 1, k],
            x_sem.at[1, slot - 1, k],
            right if k < PIECES // 2 else left,
        )

    def relay(slot, k):
        y_copy(slot, k).wait_recv()
        if slot < 3:
            y_copy(slot + 1, k).start()
        x_copy(slot, k).start()

    for k in range(PIECES):
        y_copy(1, k).start()

    lane = lax.broadcasted_iota(jnp.int32, (LANES, LANES), 1)
    row = lax.broadcasted_iota(jnp.int32, (LANES, LANES), 0)
    taps_r[...] = jnp.take_along_axis(lt_ref[...].T, (LANES - lane) % LANES, axis=1)

    def build(g, carry):
        spread = jnp.broadcast_to(taps_r[pl.ds(g, 1), :], (LANES, LANES))
        circ = pltpu.roll(spread, 0, 1, stride=1, stride_axis=0)
        high = circ.astype(BF16).astype(F32)
        low = circ - high
        below = lane <= row
        zero = jnp.zeros_like(circ)
        toep[g, :, 0:128] = jnp.where(below, zero, high).astype(BF16)
        toep[g, :, 128:256] = jnp.where(below, high, zero).astype(BF16)
        toep[g, :, 256:384] = jnp.where(below, zero, low).astype(BF16)
        toep[g, :, 384:512] = jnp.where(below, low, zero).astype(BF16)
        return carry

    lax.fori_loop(0, channels // GROUP, build, 0)

    taps_s[...] = jnp.zeros_like(taps_s)
    taps_s[0 : st_ref.shape[0], :] = st_ref[...]

    @pl.when(seq == 0)
    def _():
        fhalo[...] = jnp.zeros_like(fhalo)
        phalo[...] = jnp.zeros_like(phalo)

    feat_copy.wait()

    @pl.when(has_prev)
    def _():
        feature_halo.wait_recv()

    def short(part, b):
        start = pl.multiple_of(part * channels + b * LANES, LANES)
        groups = taps_s[:, part * LANES : (part + 1) * LANES]
        index = b * per_block + lane[0:8] // GROUP
        taps = jnp.take_along_axis(groups, index, axis=1)
        own = feat[:, pl.ds(start, LANES)].astype(F32)
        before = fhalo[:, pl.ds(start, LANES)].astype(F32)
        joined = jnp.concatenate([before[halo_rows - 8 :], own], axis=0)
        total = taps[0:1] * own
        for j in range(1, st_ref.shape[0]):
            total = total + taps[j : j + 1] * pltpu.roll(joined, j, 0)[8:]
        return total

    def short_block(b, carry):
        at = pl.ds(pl.multiple_of(b * LANES, LANES), LANES)
        qf[:, at] = short(0, b)
        pown[:, at] = (short(1, b) * short(2, b)).astype(BF16)
        return carry

    def product_copy(k):
        at = pl.ds(chunk * k, chunk)
        return remote(
            pown.at[:, at], phalo.at[:, at], ph_sem.at[0, k], ph_sem.at[1, k], following
        )

    early = {1: [(1, 0)], 3: [(1, 1), (2, 0)]}
    for k in range(CHUNKS):
        lax.fori_loop(k * blocks, (k + 1) * blocks, short_block, 0)

        @pl.when(has_next)
        def _():
            product_copy(k).start()

        for slot, piece_index in early.get(k, []):
            relay(slot, piece_index)

    def long_block(b, carry):
        at = pl.ds(pl.multiple_of(b * LANES, LANES), LANES)
        past = phalo[:, at]
        here = pown[:, at]
        stack = jnp.concatenate([past, here, past, here], axis=0)
        matrix = toep[pl.ds(b * per_block, per_block)].reshape(per_block * rows, 4 * LANES)
        every = jnp.dot(matrix, stack, preferred_element_type=F32)
        mixed = every[0:rows]
        for g in range(1, per_block):
            mixed = jnp.where(
                lane // GROUP == g, every[g * rows : (g + 1) * rows], mixed
            )
        gat[0, :, at] = (qf[:, at] * mixed).astype(BF16)
        return carry

    def gate_copy(kind, k):
        at = pl.ds(chunk * k, chunk)
        source, slot, target = ((0, 1, pool[1]), (0, 2, pool[2]), (2, 3, pool[1]))[kind]
        return remote(
            gat.at[source, :, at],
            gat.at[slot, :, at],
            g_sem.at[0, kind, k],
            g_sem.at[1, kind, k],
            target,
        )

    middle = {0: [(1, 2), (2, 1)], 1: [(1, 3)], 2: [(2, 2)], 3: [(2, 3)]}
    for k in range(CHUNKS):

        @pl.when(has_prev)
        def _():
            product_copy(k).wait_recv()

        lax.fori_loop(k * blocks, (k + 1) * blocks, long_block, 0)
        gate_copy(1, k).start()
        gate_copy(0, k).start()
        for slot, piece_index in middle.get(k, []):
            relay(slot, piece_index)

    for k in range(CHUNKS):
        gate_copy(1, k).wait_recv()
        gate_copy(2, k).start()
    for k in range(CHUNKS):
        gate_copy(0, k).wait_recv()
    for k in range(CHUNKS):
        gate_copy(2, k).wait_recv()

    quarters = (y_hi, hi_outer, (y_hi - delta + 4) % 4, (y_hi + 2) % 4)

    def result_copy(slot, member):
        column = pl.multiple_of((quarters[slot] * 2 + core) * shard + half * p, half)
        return remote(
            res.at[slot, member - 1],
            out_ref.at[0, :, pl.ds(column, half)],
            o_sem.at[0, slot, member - 1],
            o_sem.at[1, slot, member - 1],
            pool[member],
        )

    late = {0: [(3, 0), (3, 1)], 1: [(3, 2)], 2: [(3, 3)]}
    for slot in range(4):
        if slot == 0:
            for copy in own_w:
                copy.wait()
        else:
            for k in range(PIECES):
                x_copy(slot, k).wait_recv()
        weights = jnp.concatenate([wbuf[slot, 0], wbuf[slot, 1]], axis=1)
        total = jnp.dot(
            gat[...].reshape(4 * rows, channels), weights, preferred_element_type=F32
        ).astype(BF16)
        for member in (3, 2, 1):
            res[slot, member - 1] = total[member * rows : (member + 1) * rows]
            result_copy(slot, member).start()
        column = pl.multiple_of((quarters[slot] * 2 + core) * shard + half * p, half)
        out_ref[0, :, pl.ds(column, half)] = total[0:rows]
        for later_slot, piece_index in late.get(slot, []):
            relay(later_slot, piece_index)

    for slot in range(4):
        for member in (3, 2, 1):
            result_copy(slot, member).wait_recv()
    for slot in range(4):
        for member in (3, 2, 1):
            result_copy(slot, member).wait_send()
    for slot in range(1, 4):
        for k in range(PIECES):
            y_copy(slot, k).wait_send()
            x_copy(slot, k).wait_send()
    for kind in range(3):
        for k in range(CHUNKS):
            gate_copy(kind, k).wait_send()

    @pl.when(has_next)
    def _():
        feature_halo.wait_send()
        for k in range(CHUNKS):
            product_copy(k).wait_send()


def on_device(seq_count, features, short_taps, long_taps, out_weight):
    rows = features.shape[1]
    channels = features.shape[2] // 3
    depth, shard = out_weight.shape
    width = shard * 8
    dma = pltpu.SemaphoreType.DMA
    whole = pl.BlockSpec(memory_space=pltpu.VMEM)
    anywhere = pl.BlockSpec(memory_space=pl.ANY)
    return pl.pallas_call(
        functools.partial(kernel, seq_count),
        out_shape=jax.ShapeDtypeStruct((1, rows, width), BF16),
        in_specs=[anywhere, whole, whole, anywhere],
        out_specs=whole,
        scratch_shapes=[
            pltpu.VMEM((rows, 3 * channels), BF16),
            pltpu.VMEM((16, 3 * channels), BF16),
            pltpu.VMEM((8, short_taps.shape[1]), F32),
            pltpu.VMEM((LANES, LANES), F32),
            pltpu.VMEM((channels // GROUP, rows, 4 * LANES), BF16),
            pltpu.VMEM((rows, channels), F32),
            pltpu.VMEM((rows, channels), BF16),
            pltpu.VMEM((rows, channels), BF16),
            pltpu.VMEM((4, 2, depth, LANES), BF16),
            pltpu.VMEM((4, rows, channels), BF16),
            pltpu.VMEM((4, 3, rows, shard // 2), BF16),
            dma((3,)),
            dma((2,)),
            dma((2, CHUNKS)),
            dma((2, 3, PIECES)),
            dma((2, 3, PIECES)),
            dma((2, 3, CHUNKS)),
            dma((2, 4, 3)),
        ],
        compiler_params=pltpu.CompilerParams(
            collective_id=0, has_side_effects=True, vmem_limit_bytes=56 * 1024 * 1024
        ),
    )(features, short_taps, long_taps, out_weight)


def solution(mesh):
    in_specs = (P("fsdp", "seq", None), P(), P(), P(None, "fsdp"))
    out_specs = P("fsdp", "seq", None)
    return jax.shard_map(
        functools.partial(on_device, mesh.shape["seq"]),
        mesh=mesh,
        in_specs=in_specs,
        out_specs=out_specs,
        check_vma=False,
    )
```

time: 505 us -> 72 us (0.14)
  the two profiles are of different devices: /device:TPU:56 before, /device:TPU:1 now
where the time goes in v1:
time: 72 us; the launch traced here: 71.9 us
  Pallas kernels  69.6 us (97%)
  local copies, waits for them, and re-layouts  2.29 us (3%)
    pallas_call x1, Pallas kernels, on_device(): pl.pallas_call(functools.partial(kernel, seq_count), out_shape=jax.ShapeD...  69.6 us
    unnamed x1, local copies, waits for them, and re-layouts  2.29 us

profile of v1, /device:TPU:1, one launch (start us, length us, event | category | flops | bytes accessed | tf_op | source)
XLA Modules:
  0.0 71.9 jit_solution(6151934428420852531)
XLA Ops:
  0.0 69.6 %shard_map.46 = bf16[1,128,4096]{2,1,0:T(8,128)(2,1)} custom-call(bf16[1,128,6144]{2,1,0:T(8,128)(2,1)} %x_hbm.1, f32[7,384]{1,0:T(8,128)} %st_ref.1, f32[128,128]{1,0:T(8,128)} %lt_ref.1, bf16[2048,512]{1,0:T(8,128)(2,1)} %w_hbm.1), custom_call_target="tpu_custom_call" | custom-call | tf_op jit(solution)/shard_map/pallas_call | solution.py:334
  69.6 2.3 %copy.6 = bf16[1,128,4096]{2,1,0:T(8,128)(2,1)} copy(bf16[1,128,4096]{2,1,0:T(8,128)(2,1)} %shard_map.46) | data formatting | bytes 2097152

commit v2 on v1

--- a/solution.py
+++ b/solution.py
@@ -14,6 +14,8 @@
 LANES = 128
 PIECES = 4
 CHUNKS = 4
+TILE = 32
+TO_RIGHT = 1
 BF16 = jnp.bfloat16
 F32 = jnp.float32
 
@@ -28,13 +30,15 @@
     feat,
     fhalo,
     taps_s,
-    taps_r,
+    tables,
     toep,
     qf,
     pown,
     phalo,
+    wown,
     wbuf,
     gat,
+    res_own,
     res,
     loc_sem,
     fh_sem,
@@ -42,6 +46,7 @@
     y_sem,
     x_sem,
     g_sem,
+    own_sem,
     o_sem,
 ):
     rows = feat.shape[0]
@@ -90,14 +95,8 @@
 
     feat_copy = pltpu.make_async_copy(x_hbm.at[0], feat, loc_sem.at[0])
     feat_copy.start()
-    own_w = []
-    for part in range(2):
-        column = pl.multiple_of(half * p + LANES * part, LANES)
-        copy = pltpu.make_async_copy(
-            w_hbm.at[:, pl.ds(column, LANES)], wbuf.at[0, part], loc_sem.at[1 + part]
-        )
-        copy.start()
-        own_w.append(copy)
+    own_w = pltpu.make_async_copy(w_hbm, wown, loc_sem.at[1])
+    own_w.start()
 
     barrier = pltpu.get_barrier_semaphore()
     greeted = (outer, sibling, right, left) + pool[1:]
@@ -125,10 +124,10 @@
             column = pl.multiple_of(half * p + LANES * u, LANES)
             src = w_hbm.at[at_rows, pl.ds(column, LANES)]
         else:
-            src = wbuf.at[slot - 1, u, at_rows]
+            src = wbuf.at[slot - 2, u, at_rows]
         return remote(
             src,
-            wbuf.at[slot, u, at_rows],
+            wbuf.at[slot - 1, u, at_rows],
             y_sem.at[0, slot - 1, k],
             y_sem.at[1, slot - 1, k],
             sibling if slot == 2 else outer,
@@ -136,13 +135,13 @@
 
     def x_copy(slot, k):
         at_rows = pl.ds(piece * k, piece)
-        block = wbuf.at[slot, u, at_rows]
+        block = wbuf.at[slot - 1, u, at_rows]
         return remote(
             block,
             block,
             x_sem.at[0, slot - 1, k],
             x_sem.at[1, slot - 1, k],
-            right if k < PIECES // 2 else left,
+            right if k >= PIECES - TO_RIGHT else left,
         )
 
     def relay(slot, k):
@@ -155,23 +154,31 @@
         y_copy(1, k).start()
 
     lane = lax.broadcasted_iota(jnp.int32, (LANES, LANES), 1)
-    row = lax.broadcasted_iota(jnp.int32, (LANES, LANES), 0)
-    taps_r[...] = jnp.take_along_axis(lt_ref[...].T, (LANES - lane) % LANES, axis=1)
+    taps_back = jnp.take_along_axis(lt_ref[...].T, (LANES - lane) % LANES, axis=1)
+    high = taps_back.astype(BF16).astype(F32)
+    low = taps_back - high
+    tables[0] = high
+    tables[1] = low
+    tables[2] = jnp.where((lane >= 1) & (lane <= TILE), pltpu.roll(low, TILE, 1), high)
+    tile_lane = lax.broadcasted_iota(jnp.int32, (TILE, LANES), 1)
+    tile_row = lax.broadcasted_iota(jnp.int32, (TILE, LANES), 0)
+    before_tile = tile_lane > tile_row
+    in_tile = ((tile_lane < TILE) & (tile_lane <= tile_row)) | (
+        (tile_lane >= TILE) & (tile_lane < 2 * TILE) & (tile_lane - TILE <= tile_row)
+    )
+
+    def circulant(table, g, keep):
+        spread = jnp.broadcast_to(tables[table, pl.ds(g, 1), :], (TILE, LANES))
+        turned = pltpu.roll(spread, 0, 1, stride=1, stride_axis=0)
+        return jnp.where(keep, turned, jnp.zeros_like(turned)).astype(BF16)
 
     def build(g, carry):
-        spread = jnp.broadcast_to(taps_r[pl.ds(g, 1), :], (LANES, LANES))
-        circ = pltpu.roll(spread, 0, 1, stride=1, stride_axis=0)
-        high = circ.astype(BF16).astype(F32)
-        low = circ - high
-        below = lane <= row
-        zero = jnp.zeros_like(circ)
-        toep[g, :, 0:128] = jnp.where(below, zero, high).astype(BF16)
-        toep[g, :, 128:256] = jnp.where(below, high, zero).astype(BF16)
-        toep[g, :, 256:384] = jnp.where(below, zero, low).astype(BF16)
-        toep[g, :, 384:512] = jnp.where(below, low, zero).astype(BF16)
+        toep[g, :, 0:128] = circulant(0, g, before_tile)
+        toep[g, :, 128:256] = circulant(1, g, before_tile)
+        toep[g, :, 256:384] = circulant(2, g, in_tile)
         return carry
 
-    lax.fori_loop(0, channels // GROUP, build, 0)
+    lax.fori_loop(0, channels // GROUP, build, 0, unroll=16)
 
     taps_s[...] = jnp.zeros_like(taps_s)
     taps_s[0 : st_ref.shape[0], :] = st_ref[...]
@@ -212,7 +219,7 @@
             pown.at[:, at], phalo.at[:, at], ph_sem.at[0, k], ph_sem.at[1, k], following
         )
 
-    early = {1: [(1, 0)], 3: [(1, 1), (2, 0)]}
+    early = {3: [(1, 0)]}
     for k in range(CHUNKS):
         lax.fori_loop(k * blocks, (k + 1) * blocks, short_block, 0)
 
@@ -225,17 +232,21 @@
 
     def long_block(b, carry):
         at = pl.ds(pl.multiple_of(b * LANES, LANES), LANES)
-        past = phalo[:, at]
-        here = pown[:, at]
-        stack = jnp.concatenate([past, here, past, here], axis=0)
-        matrix = toep[pl.ds(b * per_block, per_block)].reshape(per_block * rows, 4 * LANES)
-        every = jnp.dot(matrix, stack, preferred_element_type=F32)
-        mixed = every[0:rows]
-        for g in range(1, per_block):
-            mixed = jnp.where(
-                lane // GROUP == g, every[g * rows : (g + 1) * rows], mixed
-            )
-        gat[0, :, at] = (qf[:, at] * mixed).astype(BF16)
+        joined = jnp.concatenate([phalo[:, at], pown[:, at]], axis=0)
+        matrix = toep[pl.ds(b * per_block, per_block)].reshape(per_block * TILE, 3 * LANES)
+        matrix = matrix[:, : 2 * LANES + 2 * TILE]
+        for tile in range(0, rows, TILE):
+            before = joined[tile : tile + LANES]
+            here = joined[tile + LANES : tile + LANES + TILE]
+            stack = jnp.concatenate([before, before, here, here], axis=0)
+            every = jnp.dot(matrix, stack, preferred_element_type=F32)
+            mixed = every[0:TILE]
+            for g in range(1, per_block):
+                mixed = jnp.where(
+                    tile_lane // GROUP == g, every[g * TILE : (g + 1) * TILE], mixed
+                )
+            at_rows = pl.ds(tile, TILE)
+            gat[0, at_rows, at] = (qf[at_rows, at] * mixed).astype(BF16)
         return carry
 
     def gate_copy(kind, k):
@@ -249,7 +260,12 @@
             target,
         )
 
-    middle = {0: [(1, 2), (2, 1)], 1: [(1, 3)], 2: [(2, 2)], 3: [(2, 3)]}
+    middle = {
+        0: [(1, 1), (2, 0)],
+        1: [(1, 2), (2, 1)],
+        2: [(1, 3), (2, 2), (3, 0)],
+        3: [(2, 3)],
+    }
     for k in range(CHUNKS):
 
         @pl.when(has_prev)
@@ -259,53 +275,66 @@
         lax.fori_loop(k * blocks, (k + 1) * blocks, long_block, 0)
         gate_copy(1, k).start()
         gate_copy(0, k).start()
-        for slot, piece_index in middle.get(k, []):
+        for slot, piece_index in middle[k]:
             relay(slot, piece_index)
-
-    for k in range(CHUNKS):
-        gate_copy(1, k).wait_recv()
-        gate_copy(2, k).start()
+        if k > 0:
+            gate_copy(1, k - 1).wait_recv()
+            gate_copy(2, k - 1).start()
+
+    quarters = (y_hi, hi_outer, (y_hi - delta + 4) % 4, (y_hi + 2) % 4)
+    own_column = pl.multiple_of(fs * shard, shard)
+    own_result = remote(
+        res_own, out_ref.at[0, :, pl.ds(own_column, shard)], own_sem.at[0], own_sem.at[1], pool[1]
+    )
+
+    def result_column(slot):
+        return pl.multiple_of((quarters[slot] * 2 + core) * shard + half * p, half)
+
+    def result_copy(slot, member):
+        return remote(
+            res.at[slot - 1, member - 1],
+            out_ref.at[0, :, pl.ds(result_column(slot), half)],
+            o_sem.at[0, slot - 1, member - 1],
+            o_sem.at[1, slot - 1, member - 1],
+            pool[member],
+        )
+
+    own_w.wait()
     for k in range(CHUNKS):
         gate_copy(0, k).wait_recv()
+    total = jnp.dot(
+        gat[0:2].reshape(2 * rows, channels), wown[...], preferred_element_type=F32
+    ).astype(BF16)
+    res_own[...] = total[rows:]
+    own_result.start()
+    out_ref[0, :, pl.ds(own_column, shard)] = total[0:rows]
+
+    gate_copy(1, CHUNKS - 1).wait_recv()
+    gate_copy(2, CHUNKS - 1).start()
+    relay(3, 1)
     for k in range(CHUNKS):
         gate_copy(2, k).wait_recv()
 
-    quarters = (y_hi, hi_outer, (y_hi - delta + 4) % 4, (y_hi + 2) % 4)
-
-    def result_copy(slot, member):
-        column = pl.multiple_of((quarters[slot] * 2 + core) * shard + half * p, half)
-        return remote(
-            res.at[slot, member - 1],
-            out_ref.at[0, :, pl.ds(column, half)],
-            o_sem.at[0, slot, member - 1],
-            o_sem.at[1, slot, member - 1],
-            pool[member],
-        )
-
-    late = {0: [(3, 0), (3, 1)], 1: [(3, 2)], 2: [(3, 3)]}
-    for slot in range(4):
-        if slot == 0:
-            for copy in own_w:
-                copy.wait()
-        else:
-            for k in range(PIECES):
-                x_copy(slot, k).wait_recv()
-        weights = jnp.concatenate([wbuf[slot, 0], wbuf[slot, 1]], axis=1)
+    late = {1: [(3, 2)], 2: [(3, 3)], 3: []}
+    for slot in range(1, 4):
+        for k in range(PIECES):
+            x_copy(slot, k).wait_recv()
+        weights = jnp.concatenate([wbuf[slot - 1, 0], wbuf[slot - 1, 1]], axis=1)
         total = jnp.dot(
             gat[...].reshape(4 * rows, channels), weights, preferred_element_type=F32
         ).astype(BF16)
         for member in (3, 2, 1):
-            res[slot, member - 1] = total[member * rows : (member + 1) * rows]
+            res[slot - 1, member - 1] = total[member * rows : (member + 1) * rows]
             result_copy(slot, member).start()
-        column = pl.multiple_of((quarters[slot] * 2 + core) * shard + half * p, half)
-        out_ref[0, :, pl.ds(column, half)] = total[0:rows]
-        for later_slot, piece_index in late.get(slot, []):
+        out_ref[0, :, pl.ds(result_column(slot), half)] = total[0:rows]
+        for later_slot, piece_index in late[slot]:
             relay(later_slot, piece_index)
 
-    for slot in range(4):
+    own_result.wait()
+    for slot in range(1, 4):
         for member in (3, 2, 1):
             result_copy(slot, member).wait_recv()
-    for slot in range(4):
+    for slot in range(1, 4):
         for member in (3, 2, 1):
             result_copy(slot, member).wait_send()
     for slot in range(1, 4):
@@ -323,6 +352,10 @@
             product_copy(k).wait_send()
 
 
+def in_hbm(array):
+    return pltpu.with_memory_space_constraint(array, pltpu.HBM)
+
+
 def on_device(seq_count, features, short_taps, long_taps, out_weight):
     rows = features.shape[1]
     channels = features.shape[2] // 3
@@ -330,7 +363,7 @@
     width = shard * 8
     dma = pltpu.SemaphoreType.DMA
     whole = pl.BlockSpec(memory_space=pltpu.VMEM)
-    anywhere = pl.BlockSpec(memory_space=pl.ANY)
+    anywhere = pl.BlockSpec(memory_space=pltpu.HBM)
     return pl.pallas_call(
         functools.partial(kernel, seq_count),
         out_shape=jax.ShapeDtypeStruct((1, rows, width), BF16),
@@ -340,26 +373,29 @@
             pltpu.VMEM((rows, 3 * channels), BF16),
             pltpu.VMEM((16, 3 * channels), BF16),
             pltpu.VMEM((8, short_taps.shape[1]), F32),
-            pltpu.VMEM((LANES, LANES), F32),
-            pltpu.VMEM((channels // GROUP, rows, 4 * LANES), BF16),
+            pltpu.VMEM((3, LANES, LANES), F32),
+            pltpu.VMEM((channels // GROUP, TILE, 3 * LANES), BF16),
             pltpu.VMEM((rows, channels), F32),
             pltpu.VMEM((rows, channels), BF16),
             pltpu.VMEM((rows, channels), BF16),
-            pltpu.VMEM((4, 2, depth, LANES), BF16),
+            pltpu.VMEM((depth, shard), BF16),
+            pltpu.VMEM((3, 2, depth, LANES), BF16),
             pltpu.VMEM((4, rows, channels), BF16),
-            pltpu.VMEM((4, 3, rows, shard // 2), BF16),
-            dma((3,)),
+            pltpu.VMEM((rows, shard), BF16),
+            pltpu.VMEM((3, 3, rows, shard // 2), BF16),
+            dma((2,)),
             dma((2,)),
             dma((2, CHUNKS)),
             dma((2, 3, PIECES)),
             dma((2, 3, PIECES)),
             dma((2, 3, CHUNKS)),
-            dma((2, 4, 3)),
+            dma((2,)),
+            dma((2, 3, 3)),
         ],
         compiler_params=pltpu.CompilerParams(
-            collective_id=0, has_side_effects=True, vmem_limit_bytes=56 * 1024 * 1024
+            collective_id=0, has_side_effects=True, vmem_limit_bytes=28 * 1024 * 1024
         ),
-    )(features, short_taps, long_taps, out_weight)
+    )(in_hbm(features), short_taps, long_taps, in_hbm(out_weight))
 
 
 def solution(mesh):

time: 72 us -> 58.4 us (0.81); the launches traced: 71.9 us -> 57.5 us
  Pallas kernels: 69.6 us -> 55 us
    pallas_call x1, Pallas kernels: 69.6 us -> 55 us  [on_device(): pl.pallas_call(functools.partial(kernel, seq_count), out_shape=jax.ShapeD...]
    unnamed x1 -> x5, local copies, waits for them, and re-layouts: 2.29 us -> 2.52 us
where the time goes in v2:
time: 58.4 us; the launch traced here: 57.5 us
  Pallas kernels  55 us (94%)
  local copies, waits for them, and re-layouts  2.52 us (4%)
    pallas_call x1, Pallas kernels, on_device(): pl.pallas_call(functools.partial(kernel, seq_count), out_shape=jax.ShapeD...  55 us
    unnamed x5, local copies, waits for them, and re-layouts  2.52 us

profile of v2, /device:TPU:1, one launch (start us, length us, event | category | flops | bytes accessed | tf_op | source)
XLA Modules:
  0.0 57.5 jit_solution(13356743592333916974)
XLA Ops:
  0.0 0.0 copy-start
  0.0 0.8 %copy-done = f32[128,128]{1,0:T(8,128)S(1)} copy-done((f32[128,128]{1,0:T(8,128)S(1)}, f32[128,128]{1,0:T(8,128)}, u32[]{:S(2)}) %copy-start) | copy-done | bytes 65560
  0.8 0.0 copy-start.1
  0.8 0.7 %copy-done.1 = f32[7,384]{1,0:T(8,128)S(1)} copy-done((f32[7,384]{1,0:T(8,128)S(1)}, f32[7,384]{1,0:T(8,128)}, u32[]{:S(2)}) %copy-start.1) | copy-done | bytes 10776
  1.5 55.0 %shard_map.46 = bf16[1,128,4096]{2,1,0:T(8,128)(2,1)S(1)} custom-call(bf16[1,128,6144]{2,1,0:T(8,128)(2,1)} %x_hbm.1, f32[7,384]{1,0:T(8,128)S(1)} %copy-done.1, f32[128,128]{1,0:T(8,128)S(1)} %copy-done, bf16[2048,512]{1,0:T(8,128)(2,1)} %w_hbm.1), custom_call_target="tpu_custom_call" | custom-call | tf_op jit(solution)/shard_map/pallas_call | solution.py:367
  56.6 1.0 %copy.6 = bf16[1,128,4096]{2,1,0:T(8,128)(2,1)} copy(bf16[1,128,4096]{2,1,0:T(8,128)(2,1)S(1)} %shard_map.46) | data formatting | bytes 2097152
Async XLA Ops:
  0.0 0.8 %copy-start = (f32[128,128]{1,0:T(8,128)S(1)}, f32[128,128]{1,0:T(8,128)}, u32[]{:S(2)}) copy-start(f32[128,128]{1,0:T(8,128)} %lt_ref.1) | copy-start | bytes 196612
  0.8 0.7 %copy-start.1 = (f32[7,384]{1,0:T(8,128)S(1)}, f32[7,384]{1,0:T(8,128)}, u32[]{:S(2)}) copy-start(f32[7,384]{1,0:T(8,128)} %st_ref.1) | copy-start | bytes 32260

commit v3 on v2

--- a/solution.py
+++ b/solution.py
@@ -371,7 +371,7 @@
         out_specs=whole,
         scratch_shapes=[
             pltpu.VMEM((rows, 3 * channels), BF16),
-            pltpu.VMEM((16, 3 * channels), BF16),
+            pltpu.VMEM((8, 3 * channels), BF16),
             pltpu.VMEM((8, short_taps.shape[1]), F32),
             pltpu.VMEM((3, LANES, LANES), F32),
             pltpu.VMEM((channels // GROUP, TILE, 3 * LANES), BF16),

time: 58.4 us -> 56.1 us (0.961)
  Pallas kernels: 55 us -> 52.9 us
    pallas_call x1, Pallas kernels: 55 us -> 52.9 us  [on_device(): pl.pallas_call(functools.partial(kernel, seq_count), out_shape=jax.ShapeD...]
where the time goes in v3:
time: 56.1 us; the launch traced here: 55.5 us
  Pallas kernels  52.9 us (94%)
  local copies, waits for them, and re-layouts  2.52 us (4%)
    pallas_call x1, Pallas kernels, on_device(): pl.pallas_call(functools.partial(kernel, seq_count), out_shape=jax.ShapeD...  52.9 us
    unnamed x5, local copies, waits for them, and re-layouts  2.52 us

profile of v3, /device:TPU:1, one launch (start us, length us, event | category | flops | bytes accessed | tf_op | source)
XLA Modules:
  0.0 55.5 jit_solution(11151859616979791354)
XLA Ops:
  0.0 0.0 copy-start
  0.0 0.8 %copy-done = f32[128,128]{1,0:T(8,128)S(1)} copy-done((f32[128,128]{1,0:T(8,128)S(1)}, f32[128,128]{1,0:T(8,128)}, u32[]{:S(2)}) %copy-start) | copy-done | bytes 65560
  0.8 0.0 copy-start.1
  0.8 0.7 %copy-done.1 = f32[7,384]{1,0:T(8,128)S(1)} copy-done((f32[7,384]{1,0:T(8,128)S(1)}, f32[7,384]{1,0:T(8,128)}, u32[]{:S(2)}) %copy-start.1) | copy-done | bytes 10776
  1.5 52.9 %shard_map.46 = bf16[1,128,4096]{2,1,0:T(8,128)(2,1)S(1)} custom-call(bf16[1,128,6144]{2,1,0:T(8,128)(2,1)} %x_hbm.1, f32[7,384]{1,0:T(8,128)S(1)} %copy-done.1, f32[128,128]{1,0:T(8,128)S(1)} %copy-done, bf16[2048,512]{1,0:T(8,128)(2,1)} %w_hbm.1), custom_call_target="tpu_custom_call" | custom-call | tf_op jit(solution)/shard_map/pallas_call | solution.py:367
  54.5 1.0 %copy.6 = bf16[1,128,4096]{2,1,0:T(8,128)(2,1)} copy(bf16[1,128,4096]{2,1,0:T(8,128)(2,1)S(1)} %shard_map.46) | data formatting | bytes 2097152
Async XLA Ops:
  0.0 0.8 %copy-start = (f32[128,128]{1,0:T(8,128)S(1)}, f32[128,128]{1,0:T(8,128)}, u32[]{:S(2)}) copy-start(f32[128,128]{1,0:T(8,128)} %lt_ref.1) | copy-start | bytes 196612
  0.8 0.7 %copy-start.1 = (f32[7,384]{1,0:T(8,128)S(1)}, f32[7,384]{1,0:T(8,128)}, u32[]{:S(2)}) copy-start(f32[7,384]{1,0:T(8,128)} %st_ref.1) | copy-start | bytes 32260

commit v4 on v3

--- a/solution.py
+++ b/solution.py
@@ -14,7 +14,7 @@
 LANES = 128
 PIECES = 4
 CHUNKS = 4
-TILE = 32
+TILE = 16
 TO_RIGHT = 1
 BF16 = jnp.bfloat16
 F32 = jnp.float32

time: 56.1 us -> 56 us (level)
  no operation moved by 1% of the time
where the time goes in v4:
time: 56 us; the launch traced here: 55.3 us
  Pallas kernels  52.8 us (94%)
  local copies, waits for them, and re-layouts  2.52 us (4%)
    pallas_call x1, Pallas kernels, on_device(): pl.pallas_call(functools.partial(kernel, seq_count), out_shape=jax.ShapeD...  52.8 us
    unnamed x5, local copies, waits for them, and re-layouts  2.52 us

profile of v4, /device:TPU:1, one launch (start us, length us, event | category | flops | bytes accessed | tf_op | source)
XLA Modules:
  0.0 55.3 jit_solution(17792301621820312527)
XLA Ops:
  0.0 0.0 copy-start
  0.0 0.8 %copy-done = f32[128,128]{1,0:T(8,128)S(1)} copy-done((f32[128,128]{1,0:T(8,128)S(1)}, f32[128,128]{1,0:T(8,128)}, u32[]{:S(2)}) %copy-start) | copy-done | bytes 65560
  0.8 0.0 copy-start.1
  0.8 0.7 %copy-done.1 = f32[7,384]{1,0:T(8,128)S(1)} copy-done((f32[7,384]{1,0:T(8,128)S(1)}, f32[7,384]{1,0:T(8,128)}, u32[]{:S(2)}) %copy-start.1) | copy-done | bytes 10776
  1.5 52.8 %shard_map.46 = bf16[1,128,4096]{2,1,0:T(8,128)(2,1)S(1)} custom-call(bf16[1,128,6144]{2,1,0:T(8,128)(2,1)} %x_hbm.1, f32[7,384]{1,0:T(8,128)S(1)} %copy-done.1, f32[128,128]{1,0:T(8,128)S(1)} %copy-done, bf16[2048,512]{1,0:T(8,128)(2,1)} %w_hbm.1), custom_call_target="tpu_custom_call" | custom-call | tf_op jit(solution)/shard_map/pallas_call | solution.py:367
  54.3 1.0 %copy.6 = bf16[1,128,4096]{2,1,0:T(8,128)(2,1)} copy(bf16[1,128,4096]{2,1,0:T(8,128)(2,1)S(1)} %shard_map.46) | data formatting | bytes 2097152
Async XLA Ops:
  0.0 0.8 %copy-start = (f32[128,128]{1,0:T(8,128)S(1)}, f32[128,128]{1,0:T(8,128)}, u32[]{:S(2)}) copy-start(f32[128,128]{1,0:T(8,128)} %lt_ref.1) | copy-start | bytes 196612
  0.8 0.7 %copy-start.1 = (f32[7,384]{1,0:T(8,128)S(1)}, f32[7,384]{1,0:T(8,128)}, u32[]{:S(2)}) copy-start(f32[7,384]{1,0:T(8,128)} %st_ref.1) | copy-start | bytes 32260
